TPU v7x, 32 devices: a whole 2x2x4 slice. The times are simulated.
32 devices in a mesh: experts: 4 (over z), context: 4 (over y, x), dp: 2 (over core).
Axes of the slice: x: 2, y: 2, z: 4, core: 2. Of those that a mesh axis runs over, the one named last changes fastest.
Arguments:
- tokens: bfloat16 [8, 4096, 512], P(('experts', 'dp'), 'context'), may hold values from -6 to 6
- attn_gain: float32 [512], replicated, may hold values from 0.5 to 1.5
- mix_gain: float32 [512], replicated, may hold values from 0.5 to 1.5
- query_key_value_weight: bfloat16 [512, 1536], replicated, may hold values from -0.375 to 0.375
- output_weight: bfloat16 [512, 512], replicated, may hold values from -0.75 to 0.75
- router_weight: bfloat16 [512, 8], replicated, may hold values from -0.1875 to 0.1875
- w_in: bfloat16 [8, 512, 2048], P('experts'), may hold values from -1.5 to 1.5
- w_exp_out: bfloat16 [8, 2048, 512], P('experts'), may hold values from -1 to 1
- out_grad: bfloat16 [8, 4096, 512], P(('experts', 'dp'), 'context'), may hold values from -6 to 6
- group_slot: int32 [8, 4096], P(('experts', 'dp'), 'context'), may hold values from 0 to 1023, as said below
- group_routes: int32 [1024, 4], P(('experts', 'context', 'dp')), may hold values from 0 to 7, all different within a row
- route_order: int32 [1024, 4], P(('experts', 'context', 'dp')), may hold values from 0 to 127, as said below
Outputs:
- layer_out: bfloat16 [8, 4096, 512], P(('experts', 'dp'), 'context')
- token_grad: float32 [8, 4096, 512], P(('experts', 'dp'), 'context')
- attn_gain_grad: float32 [512], replicated
- mix_gain_grad: float32 [512], replicated
- qkv_grad: float32 [512, 1536], replicated
- out_proj_grad: float32 [512, 512], replicated
- route_grad: float32 [512, 8], replicated
- expert_in_grad: float32 [8, 512, 2048], P('experts')
- expert_out_grad: float32 [8, 2048, 512], P('experts')
Inputs may be any that keep to these rules, and one draw needn't show every extreme that they name: `group_slot`: in each run of 1024 positions c * 1024 to c * 1024 + 1023 of a sequence, every slot appears exactly once. `group_routes`: each row names 4 different experts; every expert is named by some row. `route_order`: in each aligned block of 32 rows, all 128 entries differ.
All inputs are finite; a program needn't handle non-finite values.
Results may differ from a plain program's by a relative error of at most 0.028.
Values may be sent and summed in bfloat16 or wider, within the bound.
A program may use at most 256 MiB of HBM per device.

v0:
```python
from functools import partial
import math
import jax
import jax.numpy as jnp
from jax import lax
from jax.sharding import PartitionSpec as P

HEADS = 8
NORM_EPS = 1e-05
MASKED = -1e30


def passed_along(block, axis, distance):
    devices = range(lax.axis_size(axis))
    route = [((i - distance) % len(devices), i) for i in devices]
    return lax.ppermute(block, axis, route)


def smooth_gate(values):
    return jax.nn.gelu(values, approximate=True)


def norm_forward(values, gain):
    inv_rms = lax.rsqrt(jnp.mean(values * values, axis=-1, keepdims=True) + NORM_EPS)
    return (values * inv_rms * gain, inv_rms)


def norm_backward(values, inv_rms, gain, grad_normed):
    normed = values * inv_rms
    scaled_grad = grad_normed * gain
    gain_grad = jnp.sum(grad_normed * normed, axis=0)
    inner_mean = jnp.mean(scaled_grad * normed, axis=-1, keepdims=True)
    return (inv_rms * (scaled_grad - normed * inner_mean), gain_grad)


def place_pairs(route_flat, order_flat, capacity, experts):
    same_expert = route_flat[:, None] == route_flat[None, :]
    earlier = order_flat[None, :] < order_flat[:, None]
    ranks = jnp.sum((same_expert & earlier).astype(jnp.int32), axis=1)
    return jnp.where(ranks < capacity, route_flat * capacity + ranks, experts * capacity)


def split_heads(matrix, head_count):
    return matrix.reshape(matrix.shape[0], head_count, matrix.shape[1] // head_count)


def fold_keys(carried_in, keyval, first_key, queries, first_query, block_keys):
    half_width = keyval.shape[1] // 2
    head_count = queries.shape[1]
    query_rows = queries.shape[0]
    score_scale = queries.shape[2] ** (-0.5)
    query_pos = first_query + jnp.arange(query_rows)
    block_count = jnp.clip(
        (first_query + query_rows + block_keys - 1) // block_keys, 0, keyval.shape[0] // block_keys
    )

    def fold_visit_block(step_index, carried):
        run_peak, run_total, run_accum = carried
        kv_block = lax.dynamic_slice_in_dim(keyval, step_index * block_keys, block_keys, 0)
        key_heads = split_heads(kv_block[:, :half_width], head_count)
        value_heads = split_heads(kv_block[:, half_width:], head_count)
        scores = (
            jnp.einsum("qhd,khd->hqk", queries, key_heads, preferred_element_type=jnp.float32)
            * score_scale
        )
        key_pos = step_index * block_keys + jnp.arange(block_keys)
        allowed = key_pos[None, None, :] <= query_pos[None, :, None]
        scores = jnp.where(allowed, scores, MASKED)
        new_peak = jnp.maximum(run_peak, jnp.max(scores, axis=-1))
        weights = jnp.where(allowed, jnp.exp(scores - new_peak[:, :, None]), 0.0)
        factor = jnp.exp(run_peak - new_peak)
        run_total = run_total * factor + jnp.sum(weights, axis=-1)
        update = jnp.einsum(
            "hqk,khd->qhd",
            weights.astype(jnp.bfloat16),
            value_heads,
            preferred_element_type=jnp.float32,
        )
        run_accum = run_accum * jnp.transpose(factor)[:, :, None] + update
        return (new_peak, run_total, run_accum)

    return lax.fori_loop(0, block_count, fold_visit_block, carried_in)


def back_keys(gathered, queries, grad_heads, delta_rows, log_total, first_query, block_keys):
    half_width = gathered.shape[1] // 2
    head_count = queries.shape[1]
    query_rows = queries.shape[0]
    score_scale = queries.shape[2] ** (-0.5)
    query_pos = first_query + jnp.arange(query_rows)
    block_count = (first_query + query_rows + block_keys - 1) // block_keys

    def back_visit_block(step_index, carried):
        grad_query, grad_keyval = carried
        kv_block = lax.dynamic_slice_in_dim(gathered, step_index * block_keys, block_keys, 0)
        key_heads = split_heads(kv_block[:, :half_width], head_count)
        value_heads = split_heads(kv_block[:, half_width:], head_count)
        scores = (
            jnp.einsum("qhd,khd->hqk", queries, key_heads, preferred_element_type=jnp.float32)
            * score_scale
        )
        key_pos = step_index * block_keys + jnp.arange(block_keys)
        allowed = key_pos[None, None, :] <= query_pos[None, :, None]
        probs_full = jnp.where(allowed, jnp.exp(scores - log_total[:, :, None]), 0.0)
        grad_value = jnp.einsum(
            "hqk,qhd->khd",
            probs_full.astype(jnp.bfloat16),
            grad_heads,
            preferred_element_type=jnp.float32,
        )
        grad_probs = jnp.einsum(
            "qhd,khd->hqk", grad_heads, value_heads, preferred_element_type=jnp.float32
        )
        grad_scores = (probs_full * (grad_probs - delta_rows[:, :, None])).astype(jnp.bfloat16)
        grad_query = (
            grad_query
            + jnp.einsum("hqk,khd->qhd", grad_scores, key_heads, preferred_element_type=jnp.float32)
            * score_scale
        )
        grad_key = (
            jnp.einsum("hqk,qhd->khd", grad_scores, queries, preferred_element_type=jnp.float32)
            * score_scale
        )
        merged = jnp.concatenate(
            [grad_key.reshape(block_keys, half_width), grad_value.reshape(block_keys, half_width)],
            axis=1,
        )
        grad_keyval = lax.dynamic_update_slice_in_dim(
            grad_keyval, merged, step_index * block_keys, 0
        )
        return (grad_query, grad_keyval)

    initial = (jnp.zeros(queries.shape, jnp.float32), jnp.zeros(gathered.shape, jnp.float32))
    return lax.fori_loop(0, block_count, back_visit_block, initial)


def per_device(
    tokens,
    attn_gain,
    mix_gain,
    query_key_value_weight,
    output_weight,
    router_weight,
    w_in,
    w_exp_out,
    out_grad,
    group_slot,
    group_routes,
    route_order,
):
    query_rows = tokens.shape[1]
    model_width = tokens.shape[2]
    head_count = HEADS
    head_size = model_width // head_count
    block_keys = math.gcd(query_rows, 512)
    first_query = lax.axis_index("context") * query_rows
    inputs = tokens[0].astype(jnp.float32)
    normed_one, inv_rms_one = norm_forward(inputs, attn_gain)
    act_low = normed_one.astype(jnp.bfloat16)
    qkv_low = jnp.dot(act_low, query_key_value_weight, preferred_element_type=jnp.float32).astype(
        jnp.bfloat16
    )
    queries = split_heads(qkv_low[:, :model_width], head_count)
    keyval = qkv_low[:, model_width:]
    initial = (
        jnp.full((head_count, query_rows), MASKED, jnp.float32),
        jnp.zeros((head_count, query_rows), jnp.float32),
        jnp.zeros((query_rows, head_count, head_size), jnp.float32),
    )
    fold_local = partial(fold_keys, queries=queries, first_query=first_query, block_keys=block_keys)
    run_peak, run_total, run_accum = fold_local(
        initial, lax.all_gather(keyval, "context", axis=0, tiled=True), jnp.int32(0)
    )
    attn_heads = run_accum / jnp.transpose(run_total)[:, :, None]
    log_total = run_peak + jnp.log(run_total)
    attention_reduced = attn_heads.reshape(query_rows, model_width).astype(jnp.bfloat16)
    residual = inputs + jnp.dot(
        attention_reduced, output_weight, preferred_element_type=jnp.float32
    )
    normed_two, inv_rms_two = norm_forward(residual, mix_gain)
    mixing_input = normed_two.astype(jnp.bfloat16)
    mixing_logits = jnp.dot(mixing_input, router_weight, preferred_element_type=jnp.float32)
    slot_row = group_slot[0]
    inverse = (
        jnp.zeros((query_rows,), jnp.int32)
        .at[slot_row]
        .set(jnp.arange(query_rows, dtype=jnp.int32))
    )
    groups, top_count = group_routes.shape
    experts = router_weight.shape[1]
    members = query_rows // groups
    capacity = 5 * groups * top_count // (4 * experts)
    local_experts = w_in.shape[0]
    sources = experts // local_experts
    slot_total = experts * capacity
    grouped_in = mixing_input[inverse].reshape(groups, members, model_width)
    grouped_logit = mixing_logits[inverse].reshape(groups, members, experts)
    route_index = jnp.broadcast_to(group_routes[:, None, :], (groups, members, top_count))
    chosen = jnp.take_along_axis(grouped_logit, route_index, axis=2)
    weights = jax.nn.softmax(chosen, axis=1)
    mix_low = weights.astype(jnp.bfloat16)
    mixed_rows = jnp.einsum(
        "gtk,gtd->gkd", mix_low, grouped_in, preferred_element_type=jnp.float32
    ).astype(jnp.bfloat16)
    pair_index = place_pairs(group_routes.reshape(-1), route_order.reshape(-1), capacity, experts)
    send_rows = (
        jnp.zeros((slot_total + 1, model_width), jnp.bfloat16)
        .at[pair_index]
        .set(mixed_rows.reshape(-1, model_width))
    )
    received = lax.all_to_all(
        send_rows[:slot_total].reshape(experts, capacity, model_width),
        "experts",
        split_axis=0,
        concat_axis=0,
        tiled=True,
    )
    received = received.reshape(sources, local_experts, capacity, model_width)
    pre_act = jnp.einsum("secd,edh->sech", received, w_in, preferred_element_type=jnp.float32)
    hidden_act, gate_pull = jax.vjp(smooth_gate, pre_act)
    hidden_low = hidden_act.astype(jnp.bfloat16)
    expert_res = jnp.einsum(
        "sech,ehd->secd", hidden_low, w_exp_out, preferred_element_type=jnp.float32
    ).astype(jnp.bfloat16)
    returned = lax.all_to_all(
        expert_res.reshape(experts, capacity, model_width),
        "experts",
        split_axis=0,
        concat_axis=0,
        tiled=True,
    )
    zero_row = jnp.zeros((1, model_width), jnp.bfloat16)
    outputs = jnp.concatenate([returned.reshape(slot_total, model_width), zero_row], axis=0)[
        pair_index
    ]
    outputs = outputs.reshape(groups, top_count, model_width)
    combined = jnp.einsum(
        "gtk,gkd->gtd", mix_low, outputs, preferred_element_type=jnp.float32
    ).reshape(query_rows, model_width)
    layer_out = (residual + combined[slot_row]).astype(jnp.bfloat16)
    grad_top = out_grad[0]
    grouped_grad = grad_top[inverse].reshape(groups, members, model_width)
    grad_w_comb = jnp.einsum(
        "gtd,gkd->gtk", grouped_grad, outputs, preferred_element_type=jnp.float32
    )
    grad_out_rows = jnp.einsum(
        "gtk,gtd->gkd", mix_low, grouped_grad, preferred_element_type=jnp.float32
    ).astype(jnp.bfloat16)
    grad_send = (
        jnp.zeros((slot_total + 1, model_width), jnp.bfloat16)
        .at[pair_index]
        .set(grad_out_rows.reshape(-1, model_width))
    )
    grad_recv = lax.all_to_all(
        grad_send[:slot_total].reshape(experts, capacity, model_width),
        "experts",
        split_axis=0,
        concat_axis=0,
        tiled=True,
    )
    grad_recv = grad_recv.reshape(sources, local_experts, capacity, model_width)
    w_exp_out_grad = jnp.einsum(
        "sech,secd->ehd", hidden_low, grad_recv, preferred_element_type=jnp.float32
    )
    grad_hidden = jnp.einsum(
        "secd,ehd->sech", grad_recv, w_exp_out, preferred_element_type=jnp.float32
    )
    grad_pre = gate_pull(grad_hidden)[0].astype(jnp.bfloat16)
    w_in_grad = jnp.einsum("secd,sech->edh", received, grad_pre, preferred_element_type=jnp.float32)
    grad_owner = jnp.einsum(
        "sech,edh->secd", grad_pre, w_in, preferred_element_type=jnp.float32
    ).astype(jnp.bfloat16)
    grad_back = lax.all_to_all(
        grad_owner.reshape(experts, capacity, model_width),
        "experts",
        split_axis=0,
        concat_axis=0,
        tiled=True,
    )
    grad_mixed = jnp.concatenate([grad_back.reshape(slot_total, model_width), zero_row], axis=0)[
        pair_index
    ]
    grad_mixed = grad_mixed.reshape(groups, top_count, model_width)
    grad_w_mix = jnp.einsum(
        "gkd,gtd->gtk", grad_mixed, grouped_in, preferred_element_type=jnp.float32
    )
    grad_members = jnp.einsum(
        "gtk,gkd->gtd", mix_low, grad_mixed, preferred_element_type=jnp.float32
    )
    grad_weights = grad_w_comb + grad_w_mix
    grad_chosen = weights * (grad_weights - jnp.sum(weights * grad_weights, axis=1, keepdims=True))
    route_onehot = (group_routes[:, :, None] == jnp.arange(experts)[None, None, :]).astype(
        jnp.float32
    )
    grad_grouped = jnp.einsum(
        "gtk,gke->gte", grad_chosen, route_onehot, precision=lax.Precision.HIGHEST
    ).astype(jnp.bfloat16)
    grad_logits = grad_grouped.reshape(query_rows, experts)[slot_row]
    route_grad = jnp.einsum(
        "td,te->de", mixing_input, grad_logits, preferred_element_type=jnp.float32
    )
    grad_mix = grad_members.reshape(query_rows, model_width)[slot_row] + jnp.einsum(
        "te,de->td", grad_logits, router_weight, preferred_element_type=jnp.float32
    )
    grad_norm_two, mix_gain_grad = norm_backward(residual, inv_rms_two, mix_gain, grad_mix)
    grad_residual = grad_top.astype(jnp.float32) + grad_norm_two
    grad_proj = grad_residual.astype(jnp.bfloat16)
    out_proj_grad = jnp.einsum(
        "td,te->de", attention_reduced, grad_proj, preferred_element_type=jnp.float32
    )
    grad_att = jnp.einsum(
        "te,de->td", grad_proj, output_weight, preferred_element_type=jnp.float32
    ).astype(jnp.bfloat16)
    grad_heads = split_heads(grad_att, head_count)
    delta_rows = jnp.transpose(jnp.sum(grad_heads.astype(jnp.float32) * attn_heads, axis=-1))
    keys_back = lax.all_gather(keyval, "context", axis=0, tiled=True)
    grad_query, grad_keyval = back_keys(
        keys_back, queries, grad_heads, delta_rows, log_total, first_query, block_keys
    )
    cycle_size = lax.axis_size("context")
    own_index = lax.axis_index("context")

    def take_block(block_id):
        return lax.dynamic_slice_in_dim(grad_keyval, block_id * query_rows, query_rows, 0)

    def pass_on(step_index, carried):
        moved = passed_along(carried.astype(jnp.bfloat16), "context", 1).astype(carried.dtype)
        block_id = (own_index - 2 - step_index + 2 * cycle_size) % cycle_size
        return moved + take_block(block_id)

    start_block = take_block((own_index - 1 + cycle_size) % cycle_size)
    own_keyval = lax.fori_loop(0, cycle_size - 1, pass_on, start_block)
    grad_qkv = jnp.concatenate(
        [grad_query.reshape(query_rows, model_width), own_keyval], axis=1
    ).astype(jnp.bfloat16)
    qkv_grad = jnp.einsum("td,te->de", act_low, grad_qkv, preferred_element_type=jnp.float32)
    grad_act = jnp.einsum(
        "te,de->td", grad_qkv, query_key_value_weight, preferred_element_type=jnp.float32
    )
    grad_norm_one, attn_gain_grad = norm_backward(inputs, inv_rms_one, attn_gain, grad_act)
    token_grad = grad_residual + grad_norm_one
    dense_sums = lax.psum(
        (attn_gain_grad, mix_gain_grad, qkv_grad, out_proj_grad, route_grad),
        ("experts", "context", "dp"),
    )
    expert_sums = (
        lax.psum(w_in_grad.astype(jnp.bfloat16), ("context", "dp")).astype(jnp.float32),
        lax.psum(w_exp_out_grad.astype(jnp.bfloat16), ("context", "dp")).astype(jnp.float32),
    )
    return (
        layer_out[None],
        token_grad[None],
        dense_sums[0],
        dense_sums[1],
        dense_sums[2],
        dense_sums[3],
        dense_sums[4],
        expert_sums[0],
        expert_sums[1],
    )


def solution(mesh):
    return jax.shard_map(
        per_device,
        mesh=mesh,
        in_specs=(
            P(("experts", "dp"), "context", None),
            P(),
            P(),
            P(),
            P(),
            P(),
            P("experts", None, None),
            P("experts", None, None),
            P(("experts", "dp"), "context", None),
            P(("experts", "dp"), "context"),
            P(("experts", "context", "dp"), None),
            P(("experts", "context", "dp"), None),
        ),
        out_specs=(
            P(("experts", "dp"), "context", None),
            P(("experts", "dp"), "context", None),
            P(),
            P(),
            P(),
            P(),
            P(),
            P("experts", None, None),
            P("experts", None, None),
        ),
        check_vma=False,
    )
```

profile of v0, /device:TPU:0, one launch (start us, length us, event | category | flops | bytes accessed | tf_op | source)
XLA Modules:
  0.0 1068.3 jit_solution(3388636967692149106)
XLA Ops:
  23.1 4.3 scatter_custom_fusion
  27.5 6.7 gather_fusion.4
  35.6 69.2 %all-gather.2.cloned.1.call-done = bf16[4096,1024]{1,0:T(8,128)(2,1)} async-done(((bf16[1024,1024]{1,0:T(8,128)(2,1)}), bf16[4096,1024]{1,0:T(8,128)(2,1)}) %all-gather.2.cloned.1.call-update) | async-done | bytes 8388624 | tf_op jit(solution)/shard_map/all_gather | solution.py:172
  104.8 11.9 %copy.195 = bf16[4096,1024]{0,1:T(8,128)(2,1)} copy(bf16[4096,1024]{1,0:T(8,128)(2,1)} %all-gather.2.cloned.1.call-done) | data formatting | bytes 16777216
  118.3 33.6 %while.44 = (s32[]{:T(128)}, f32[8,1024]{1,0:T(8,128)S(1)}, f32[8,1024]{1,0:T(8,128)S(1)}, f32[1024,8,64]{0,2,1:T(8,128)}, s32[]{:T(128)}, /*index=5*/bf16[4096,...) while((s32[]{:T(128)}, f32[8,1024]{1,0:T(8,128)S(1)}, ...), condition=%wide.region_4.5_spmd.clone, body=%wide.region_1.4_spmd.clone.sunk | while | flops 1129866752 | bytes 78131464 | solution.py:82
  127.7 6.0 bitcast_add_fusion.5
  144.5 6.0 bitcast_add_fusion.5
  163.7 34.4 %gather_fusion.8 = f32[4096]{0:T(1024)S(1)} fusion(f32[32,32,8]{2,1,0:T(8,128)S(1)} %bitcast.226, s32[4096]{0:T(1024)S(1)} %reshape.372), kind=kCustom, calls=%fused_computation.8 | custom fusion | bytes 81920 | tf_op jit(solution)/shard_map/jit(take_along_axis)/gather | solution.py:199
  199.3 5.1 gather_fusion.1
  209.2 4.6 all-to-all-start
  216.7 4.7 all-to-all-done
  230.9 4.3 fusion.58
  241.6 4.2 all-to-all-start.1
  246.1 4.4 bitcast_convert_fusion.1
  264.8 6.9 gather_fusion.6
  279.1 4.9 multiply_reduce_fusion
  284.0 6.9 gather_fusion.3
  293.9 4.6 multiply_add_fusion.1
  301.9 7.9 broadcast_in_dim.113
  309.7 85.8 %while.45 = (s32[]{:T(128)}, f32[1024,8,64]{0,2,1:T(8,128)}, f32[4096,1024]{0,1:T(8,128)}, s32[]{:T(128)}, bf16[4096,1024]{0,1:T(8,128)(2,1)}, /*index=5*/bf16[1...) while((s32[]{:T(128)}, f32[1024,8,64]{0,2,1:T(8,128)}, ...), condition=%wide.region_16.17_spmd.clone, body=%wide.region_15.16_spmd.clone.sunk | while | flops 2728658432 | bytes 154251664 | solution.py:134
  311.4 8.1 fusion.196
  320.0 9.3 fusion.197
  334.0 10.3 fusion.198
  344.3 6.1 convolution_multiply_fusion.2
  353.3 8.8 fusion.196
  362.5 9.5 fusion.197
  376.7 11.0 %fusion.198 = f32[8,512,64]{1,2,0:T(8,128)} fusion(bf16[1024,8,64]{0,2,1:T(8,128)(2,1)} %get-tuple-element.733, f32[8,512,1024]{2,1,0:T(8,128)} %fusion.196, f32[8,1024]{1,0:T(8,128)S(1)} %get-tuple-element.732, pred[1024,512]{0,1:T(8,128)(4,1)S(1)} %broadcast_compare_fusion.6), kind=kOutput, calls=%fused_computation.38.clone.1 | convolution fusion | flops 553648128 | bytes 19431424 | tf_op jit(solution)/shard_map/while/body/hqk,qhd->khd/dot_general | solution.py:105
  387.7 6.2 convolution_multiply_fusion.2
  399.4 4.1 copy.223
  412.0 498.4 %while.43 = (s32[]{:T(128)}, bf16[1024,1024]{1,0:T(8,128)(2,1)}, s32[]{:T(128)}, f32[4096,1024]{0,1:T(8,128)}, s32[]{:T(128)}, /*index=5*/s32[]{:T(128)}, s32[]{...) while((s32[]{:T(128)}, bf16[1024,1024]{1,0:T(8,128)(2,1)}, s32[]{:T(128)}, ...), condition=%wide.region_18.19_spmd, body=%wide.region_17.18_spmd.sunk | while | flops 3145747 | bytes 33554764 | solution.py:332
  412.0 120.4 %collective-permute-start = (bf16[1024,1024]{1,0:T(8,128)(2,1)}, bf16[1024,1024]{1,0:T(8,128)(2,1)}, u32[]{:S(2)}, u32[]{:S(2)}) collective-permute-start(bf16[1024,1024]{1,0:T(8,128)(2,1)} %get-tuple-element.753), channel_id=1, source_target_pairs={{6,0},{0,2},{2,4},{4,6},{7,1},{1,3},{3,5},{5,7},{14,8},{8,10},{10,... | collective-permute-start | bytes 6291464 | tf_op jit(solution)/shard_map/while/body/eval_jaxpr/ppermute | solution.py:16
  532.3 4.8 constant_dynamic-slice_fusion.5
  537.1 5.3 copy.266
  542.5 265.3 %collective-permute-done = bf16[1024,1024]{1,0:T(8,128)(2,1)} collective-permute-done((bf16[1024,1024]{1,0:T(8,128)(2,1)}, bf16[1024,1024]{1,0:T(8,128)(2,1)}, u32[]{:S(2)}, u32[]{:S(2)}) %collective-permute-start) | collective-permute-done | bytes 2097184 | tf_op jit(solution)/shard_map/while/body/eval_jaxpr/ppermute | solution.py:16
  807.8 5.0 convert_add_fusion.3
  812.7 4.8 constant_dynamic-slice_fusion.5
  817.5 5.3 copy.266
  822.9 34.2 %collective-permute-done = bf16[1024,1024]{1,0:T(8,128)(2,1)} collective-permute-done((bf16[1024,1024]{1,0:T(8,128)(2,1)}, bf16[1024,1024]{1,0:T(8,128)(2,1)}, u32[]{:S(2)}, u32[]{:S(2)}) %collective-permute-start) | collective-permute-done | bytes 2097184 | tf_op jit(solution)/shard_map/while/body/eval_jaxpr/ppermute | solution.py:16
  857.0 5.0 convert_add_fusion.3
  862.0 4.8 constant_dynamic-slice_fusion.5
  866.8 5.3 copy.266
  872.1 33.2 %collective-permute-done = bf16[1024,1024]{1,0:T(8,128)(2,1)} collective-permute-done((bf16[1024,1024]{1,0:T(8,128)(2,1)}, bf16[1024,1024]{1,0:T(8,128)(2,1)}, u32[]{:S(2)}, u32[]{:S(2)}) %collective-permute-start) | collective-permute-done | bytes 2097184 | tf_op jit(solution)/shard_map/while/body/eval_jaxpr/ppermute | solution.py:16
  905.4 5.0 convert_add_fusion.3
  910.4 5.4 fusion.50
  927.4 40.2 %all-reduce.2 = (f32[512]{0:T(512)}, f32[512]{0:T(512)}, f32[512,8]{0,1:T(8,128)}) all-reduce(f32[512]{0:T(512)S(1)} %get-tuple-element.429, f32[512]{0:T(512)S(1)} %copy-done.56, f32[512,8]{0,1:T(8,128)S(1)} %fusion.116), channel_id=1, replica_groups=mesh['experts'=4,'context'=4,'dp'=2] {'experts','context','dp'}, use_global_device_ids=true, to_apply=%region_21.22 | all-reduce | flops 5120 | bytes 40960 | tf_op jit(solution)/shard_map/psum | solution.py:342
  967.5 6.8 convert_element_type.136
  974.3 4.6 convert_element_type.138
  978.9 77.8 %all-reduce.8.cloned.1.call-done = (f32[512,1536]{1,0:T(8,128)}, f32[512,512]{1,0:T(8,128)}) async-done(((f32[512,1536]{1,0:T(8,128)}, f32[512,512]{1,0:T(8,128)}), (f32[512,1536]{1,0:T(8,128)}, f32[512,512]{1,0:T(8,128)})) %all-reduce.8.cloned.1.call-update) | async-done | bytes 4194320 | tf_op jit(solution)/shard_map/psum | solution.py:342
  (277 shorter events, 148.9 us)
Async XLA Ops:
  7.2 97.6 %all-gather.2.cloned.1.call-start = ((), (), s32[]{:S(2)}) async-start(), calls=%async_computation.4 | async-start | bytes 10485760 | tf_op jit(solution)/shard_map/all_gather | solution.py:172
  14.4 3.8 copy-start.50
  16.7 3.9 copy-start.61
  18.2 5.0 copy-start.58
  18.3 16.0 %copy-start.43 = (s32[32,4]{1,0:T(8,128)}, s32[32,4]{1,0:T(8,128)S(1)}, u32[]{:S(2)}) copy-start(s32[32,4]{1,0:T(8,128)S(1)} %copy.198) | copy-start | bytes 1540
  27.5 133.4 %copy-start.45 = (s32[1024]{0:T(1024)}, s32[1024]{0:T(1024)S(1)}, u32[]{:S(2)}) copy-start(s32[1024]{0:T(1024)S(1)} %fusion.96) | copy-start | bytes 12292
  34.4 82.3 %copy-start.62 = (s32[128]{0:T(128)}, s32[128]{0:T(128)S(1)}, u32[]{:S(2)}) copy-start(s32[128]{0:T(128)S(1)} %fusion.101) | copy-start | bytes 1540
  123.6 4.1 copy-start.11
  140.4 4.1 copy-start.11
  163.7 35.2 %copy-start.46 = (s32[1024]{0:T(1024)S(1)}, s32[1024]{0:T(1024)}, u32[]{:S(2)}) copy-start(s32[1024]{0:T(1024)} %copy-done.45) | copy-start | bytes 12292
  199.3 5.1 copy-start.44
  199.3 5.1 copy-start.55
  199.3 5.1 copy-start.57
  204.3 9.5 copy-start.20
  207.2 8.8 copy-start.26
  207.2 8.8 copy-start.32
  209.2 12.1 %all-to-all-start = ((bf16[8,20,512]{2,1,0:T(8,128)(2,1)}), bf16[8,20,512]{2,1,0:T(8,128)(2,1)S(1)}, u32[]{:S(2)}, u32[]{:S(2)}) async-start(bf16[8,20,512]{2,1,0:T(8,128)(2,1)} %reshape.290), calls=%async_computation | async-start | bytes 393216 | tf_op jit(solution)/shard_map/all_to_all | solution.py:211
  221.3 9.6 all-to-all-start.2
  224.7 4.3 copy-start.63
  230.9 4.3 copy-start.24
  241.6 10.5 all-to-all-start.1
  245.9 721.7 %all-reduce.10.cloned.1.call-start = ((), (), s32[]{:S(2)}) async-start(), calls=%async_computation.6 | async-start | bytes 16777216 | tf_op jit(solution)/shard_map/psum | solution.py:347
  252.1 9.8 all-to-all-start.3
  255.7 801.1 %all-reduce.8.cloned.1.call-start = ((), (), s32[]{:S(2)}) async-start(), calls=%async_computation.5 | async-start | bytes 8388608 | tf_op jit(solution)/shard_map/psum | solution.py:342
  275.1 3.9 copy-start.41
  275.1 3.9 copy-start.48
  275.1 3.9 copy-start.52
  279.1 4.9 copy-start.33
  293.9 4.6 copy-start.13
  293.9 4.6 copy-start.36
  301.9 7.9 copy-start.3
  301.9 7.9 copy-start.49
  311.4 8.5 copy-start.38
  320.0 9.3 copy-start.4
  344.3 6.1 copy-start.10
  353.3 9.2 copy-start.38
  362.5 9.5 copy-start.4
  387.7 6.2 copy-start.10
  403.5 5.1 copy-start.22
  411.9 498.4 %copy-start.17 = (bf16[1,1024,512]{1,2,0:T(8,128)(2,1)S(1)}, bf16[1,1024,512]{1,2,0:T(8,128)(2,1)}, u32[]{:S(2)}) copy-start(bf16[1,1024,512]{1,2,0:T(8,128)(2,1)} %copy-done.15) | copy-start | bytes 3145732
  411.9 498.4 %copy-start.54 = (f32[1024]{0:T(1024)S(1)}, f32[1024]{0:T(1024)}, u32[]{:S(2)}) copy-start(f32[1024]{0:T(1024)} %copy-done.53) | copy-start | bytes 12292
  411.9 498.4 %copy-start.60 = (f32[512]{0:T(512)S(1)}, f32[512]{0:T(512)}, u32[]{:S(2)}) copy-start(f32[512]{0:T(512)} %param.19) | copy-start | bytes 6148
  412.0 395.8 %collective-permute-start = (bf16[1024,1024]{1,0:T(8,128)(2,1)}, bf16[1024,1024]{1,0:T(8,128)(2,1)}, u32[]{:S(2)}, u32[]{:S(2)}) collective-permute-start(bf16[1024,1024]{1,0:T(8,128)(2,1)} %get-tuple-element.753), channel_id=1, source_target_pairs={{6,0},{0,2},{2,4},{4,6},{7,1},{1,3},{3,5},{5,7},{14,8},{8,10},{10,... | collective-permute-start | bytes 6291464 | tf_op jit(solution)/shard_map/while/body/eval_jaxpr/ppermute | solution.py:16
  812.7 44.3 %collective-permute-start = (bf16[1024,1024]{1,0:T(8,128)(2,1)}, bf16[1024,1024]{1,0:T(8,128)(2,1)}, u32[]{:S(2)}, u32[]{:S(2)}) collective-permute-start(bf16[1024,1024]{1,0:T(8,128)(2,1)} %get-tuple-element.753), channel_id=1, source_target_pairs={{6,0},{0,2},{2,4},{4,6},{7,1},{1,3},{3,5},{5,7},{14,8},{8,10},{10,... | collective-permute-start | bytes 6291464 | tf_op jit(solution)/shard_map/while/body/eval_jaxpr/ppermute | solution.py:16
  862.0 43.4 %collective-permute-start = (bf16[1024,1024]{1,0:T(8,128)(2,1)}, bf16[1024,1024]{1,0:T(8,128)(2,1)}, u32[]{:S(2)}, u32[]{:S(2)}) collective-permute-start(bf16[1024,1024]{1,0:T(8,128)(2,1)} %get-tuple-element.753), channel_id=1, source_target_pairs={{6,0},{0,2},{2,4},{4,6},{7,1},{1,3},{3,5},{5,7},{14,8},{8,10},{10,... | collective-permute-start | bytes 6291464 | tf_op jit(solution)/shard_map/while/body/eval_jaxpr/ppermute | solution.py:16
  918.0 4.1 copy-start.8
  967.5 6.8 copy-start.27
  1056.8 3.8 copy-start.37
  (33 other events, 75.0 us)
Sparse Core Ops, SparseCore 0:
  14.5 90.2 all-gather.1
  250.7 227.8 all-reduce.9
  915.9 140.8 all-reduce.7
where the time goes:
time: 1080 us; the launch traced here: 1070 us
  waiting for transfers between devices  490 us (45%)
  local copies, waits for them, and re-layouts  192 us (18%)
  matrix products  139 us (13%)
  starting transfers between devices  136 us (13%)
  other arithmetic  54.6 us (5%)
  blocking collectives  40.2 us (4%)
  between operations  14.6 us (1%)
    ppermute x3, waiting for transfers between devices, passed_along(): return lax.ppermute(block, axis, route)  333 us
    ppermute x3, starting transfers between devices, passed_along(): return lax.ppermute(block, axis, route)  120 us
    psum x1, waiting for transfers between devices, per_device(): lax.psum((attn_gain_grad, mix_gain_grad, qkv_grad, out_proj_grad, route_g...  77.8 us
    all_gather x1, waiting for transfers between devices, per_device(): lax.all_gather(keyval, 'context', axis=0, tiled=True)  69.2 us
    psum x1, blocking collectives, per_device(): lax.psum((attn_gain_grad, mix_gain_grad, qkv_grad, out_proj_grad, route_g...  40.2 us
    gather x5, local copies, waits for them, and re-layouts, per_device(): chosen = jnp.take_along_axis(grouped_logit, route_index, axis=2)  35.7 us
    dynamic_slice x7, local copies, waits for them, and re-layouts, take_block(): lax.dynamic_slice_in_dim(grad_keyval, block_id * query_rows, query_rows, 0)  34.2 us
    unnamed x123, local copies, waits for them, and re-layouts  31.9 us
  transfers between devices with their start and end apart: 10, of which 9 were waited for; matrix products, arithmetic and copies ran while one was open for 24% of the time, Pallas kernels for 0%

commit v1 on v0

--- a/solution.py
+++ b/solution.py
@@ -8,6 +8,14 @@
 HEADS = 8
 NORM_EPS = 1e-05
 MASKED = -1e30
+
+
+def manage_chunk_over_axis(arr):
+    comm_axis = "experts"
+    across = ("context", "dp")
+    for nth in (across, comm_axis):
+        arr = jax.lax.psum(arr, nth)
+    return arr
 
 
 def passed_along(block, axis, distance):
@@ -339,9 +347,8 @@
     )
     grad_norm_one, attn_gain_grad = norm_backward(inputs, inv_rms_one, attn_gain, grad_act)
     token_grad = grad_residual + grad_norm_one
-    dense_sums = lax.psum(
-        (attn_gain_grad, mix_gain_grad, qkv_grad, out_proj_grad, route_grad),
-        ("experts", "context", "dp"),
+    dense_sums = manage_chunk_over_axis(
+        (attn_gain_grad, mix_gain_grad, qkv_grad, out_proj_grad, route_grad)
     )
     expert_sums = (
         lax.psum(w_in_grad.astype(jnp.bfloat16), ("context", "dp")).astype(jnp.float32),

time: 1080 us -> 1300 us (1.20)
  waiting for transfers between devices: 490 us -> 706 us
    psum x1 -> x2, waiting for transfers between devices: 77.8 us -> 217 us  [manage_chunk_over_axis(): arr = jax.lax.psum(arr, nth)]
    psum x1, waiting for transfers between devices: 0.01 us -> 77.2 us  [per_device(): lax.psum(w_in_grad.astype(jnp.bfloat16), ('context', 'dp'))]
    psum x1 -> x2, blocking collectives: 40.2 us -> 44.1 us  [manage_chunk_over_axis(): arr = jax.lax.psum(arr, nth)]
    unnamed x123 -> x127, local copies, waits for them, and re-layouts: 31.9 us -> 33.1 us
  transfers between devices with their start and end apart: 10 -> 11, of which waited for: 9 -> 11; matrix products, arithmetic and copies ran while one was open for 24% -> 8% of each run, Pallas kernels for 0% -> 0%
where the time goes in v1:
time: 1300 us; the launch traced here: 1290 us
  waiting for transfers between devices  706 us (54%)
  local copies, waits for them, and re-layouts  192 us (15%)
  matrix products  140 us (11%)
  starting transfers between devices  135 us (10%)
  other arithmetic  53.4 us (4%)
  blocking collectives  44.1 us (3%)
  between operations  14.7 us (1%)
    ppermute x3, waiting for transfers between devices, passed_along(): return lax.ppermute(block, axis, route)  334 us
    psum x2, waiting for transfers between devices, manage_chunk_over_axis(): arr = jax.lax.psum(arr, nth)  217 us
    ppermute x3, starting transfers between devices, passed_along(): return lax.ppermute(block, axis, route)  119 us
    psum x1, waiting for transfers between devices, per_device(): lax.psum(w_in_grad.astype(jnp.bfloat16), ('context', 'dp'))  77.2 us
    all_gather x1, waiting for transfers between devices, per_device(): lax.all_gather(keyval, 'context', axis=0, tiled=True)  69.2 us
    psum x2, blocking collectives, manage_chunk_over_axis(): arr = jax.lax.psum(arr, nth)  44.1 us
    gather x5, local copies, waits for them, and re-layouts, per_device(): chosen = jnp.take_along_axis(grouped_logit, route_index, axis=2)  35.7 us
    dynamic_slice x7, local copies, waits for them, and re-layouts, take_block(): lax.dynamic_slice_in_dim(grad_keyval, block_id * query_rows, query_rows, 0)  34.2 us
  transfers between devices with their start and end apart: 11, of which 11 were waited for; matrix products, arithmetic and copies ran while one was open for 8% of the time, Pallas kernels for 0%

profile of v1, /device:TPU:0, one launch (start us, length us, event | category | flops | bytes accessed | tf_op | source)
XLA Modules:
  0.0 1286.2 jit_solution(9810823839906367686)
XLA Ops:
  27.5 6.7 gather_fusion.4
  35.6 69.2 %all-gather.2.cloned.1.call-done = bf16[4096,1024]{1,0:T(8,128)(2,1)} async-done(((bf16[1024,1024]{1,0:T(8,128)(2,1)}), bf16[4096,1024]{1,0:T(8,128)(2,1)}) %all-gather.2.cloned.1.call-update) | async-done | bytes 8388624 | tf_op jit(solution)/shard_map/all_gather | solution.py:180
  104.8 11.9 copy.195
  118.3 33.6 %while.44 = (s32[]{:T(128)}, f32[8,1024]{1,0:T(8,128)S(1)}, f32[8,1024]{1,0:T(8,128)S(1)}, f32[1024,8,64]{0,2,1:T(8,128)}, s32[]{:T(128)}, /*index=5*/bf16[4096,...) while((s32[]{:T(128)}, f32[8,1024]{1,0:T(8,128)S(1)}, ...), condition=%wide.region_4.5_spmd.clone, body=%wide.region_1.4_spmd.clone.sunk | while | flops 1129866752 | bytes 78131464 | solution.py:90
  127.7 6.0 bitcast_add_fusion.5
  144.5 6.0 bitcast_add_fusion.5
  163.7 34.4 %gather_fusion.8 = f32[4096]{0:T(1024)S(1)} fusion(f32[32,32,8]{2,1,0:T(8,128)S(1)} %bitcast.226, s32[4096]{0:T(1024)S(1)} %reshape.372), kind=kCustom, calls=%fused_computation.8 | custom fusion | bytes 81920 | tf_op jit(solution)/shard_map/jit(take_along_axis)/gather | solution.py:207
  199.3 5.1 gather_fusion.1
  209.3 4.6 all-to-all-start
  216.7 4.6 all-to-all-done
  231.0 5.2 fusion.58
  259.9 6.9 gather_fusion.6
  274.2 4.9 multiply_reduce_fusion
  279.1 6.9 gather_fusion.3
  289.0 4.6 multiply_add_fusion.1
  299.0 7.9 broadcast_in_dim.113
  306.8 84.2 %while.45 = (s32[]{:T(128)}, f32[1024,8,64]{0,2,1:T(8,128)}, f32[4096,1024]{0,1:T(8,128)}, s32[]{:T(128)}, bf16[4096,1024]{0,1:T(8,128)(2,1)}, /*index=5*/bf16[1...) while((s32[]{:T(128)}, f32[1024,8,64]{0,2,1:T(8,128)}, ...), condition=%wide.region_16.17_spmd.clone, body=%wide.region_15.16_spmd.clone.sunk | while | flops 2728658432 | bytes 154251664 | solution.py:142
  308.5 8.1 fusion.196
  317.1 9.3 fusion.197
  331.1 10.3 fusion.198
  341.4 6.1 convolution_multiply_fusion.2
  350.3 8.1 fusion.196
  358.9 9.3 fusion.197
  372.9 10.3 fusion.198
  383.2 6.1 convolution_multiply_fusion.2
  401.9 497.4 %while.43 = (s32[]{:T(128)}, bf16[1024,1024]{1,0:T(8,128)(2,1)}, s32[]{:T(128)}, f32[4096,1024]{0,1:T(8,128)}, s32[]{:T(128)}, /*index=5*/s32[]{:T(128)}, s32[]{...) while((s32[]{:T(128)}, bf16[1024,1024]{1,0:T(8,128)(2,1)}, s32[]{:T(128)}, ...), condition=%wide.region_18.19_spmd, body=%wide.region_17.18_spmd.sunk | while | flops 3145747 | bytes 33554764 | solution.py:340
  401.9 118.6 %collective-permute-start = (bf16[1024,1024]{1,0:T(8,128)(2,1)}, bf16[1024,1024]{1,0:T(8,128)(2,1)}, u32[]{:S(2)}, u32[]{:S(2)}) collective-permute-start(bf16[1024,1024]{1,0:T(8,128)(2,1)} %get-tuple-element.758), channel_id=1, source_target_pairs={{6,0},{0,2},{2,4},{4,6},{7,1},{1,3},{3,5},{5,7},{14,8},{8,10},{10,... | collective-permute-start | bytes 6291464 | tf_op jit(solution)/shard_map/while/body/eval_jaxpr/ppermute | solution.py:24
  520.5 4.8 constant_dynamic-slice_fusion.5
  525.3 5.3 copy.266
  530.6 266.4 %collective-permute-done = bf16[1024,1024]{1,0:T(8,128)(2,1)} collective-permute-done((bf16[1024,1024]{1,0:T(8,128)(2,1)}, bf16[1024,1024]{1,0:T(8,128)(2,1)}, u32[]{:S(2)}, u32[]{:S(2)}) %collective-permute-start) | collective-permute-done | bytes 2097184 | tf_op jit(solution)/shard_map/while/body/eval_jaxpr/ppermute | solution.py:24
  797.1 5.0 convert_add_fusion.3
  802.0 4.8 constant_dynamic-slice_fusion.5
  806.8 5.3 copy.266
  812.2 34.0 %collective-permute-done = bf16[1024,1024]{1,0:T(8,128)(2,1)} collective-permute-done((bf16[1024,1024]{1,0:T(8,128)(2,1)}, bf16[1024,1024]{1,0:T(8,128)(2,1)}, u32[]{:S(2)}, u32[]{:S(2)}) %collective-permute-start) | collective-permute-done | bytes 2097184 | tf_op jit(solution)/shard_map/while/body/eval_jaxpr/ppermute | solution.py:24
  846.2 5.0 convert_add_fusion.3
  851.1 4.8 constant_dynamic-slice_fusion.5
  855.9 5.3 copy.266
  861.3 33.1 %collective-permute-done = bf16[1024,1024]{1,0:T(8,128)(2,1)} collective-permute-done((bf16[1024,1024]{1,0:T(8,128)(2,1)}, bf16[1024,1024]{1,0:T(8,128)(2,1)}, u32[]{:S(2)}, u32[]{:S(2)}) %collective-permute-start) | collective-permute-done | bytes 2097184 | tf_op jit(solution)/shard_map/while/body/eval_jaxpr/ppermute | solution.py:24
  894.3 5.0 convert_add_fusion.3
  899.3 5.4 fusion.50
  905.6 4.6 bitcast_convert_fusion.1
  913.8 70.2 %all-reduce.11.cloned.1.call-done = (f32[512,1536]{1,0:T(8,128)}, f32[512,512]{1,0:T(8,128)}) async-done(((f32[512,1536]{1,0:T(8,128)}, f32[512,512]{1,0:T(8,128)}), (f32[512,1536]{1,0:T(8,128)}, f32[512,512]{1,0:T(8,128)})) %all-reduce.11.cloned.1.call-update) | async-done | bytes 4194320 | tf_op jit(solution)/shard_map/psum | solution.py:17
  995.5 24.6 %all-reduce.2 = (f32[512]{0:T(512)S(1)}, f32[512]{0:T(512)S(1)}, f32[512,8]{0,1:T(8,128)S(1)}) all-reduce(f32[512]{0:T(512)S(1)} %get-tuple-element.429, f32[512]{0:T(512)S(1)} %copy-done.58, f32[512,8]{0,1:T(8,128)S(1)} %fusion.116), channel_id=1, replica_groups=mesh['experts'=4,'context'=4,'dp'=2] {'context','dp'}, use_global_device_ids=true, to_apply=%region_21.22 | all-reduce | flops 5120 | bytes 40960 | tf_op jit(solution)/shard_map/psum | solution.py:17
  1020.1 19.6 %all-reduce.4 = (f32[512]{0:T(512)}, f32[512]{0:T(512)}, f32[512,8]{0,1:T(8,128)}) all-reduce(f32[512]{0:T(512)S(1)} %get-tuple-element.475, f32[512]{0:T(512)S(1)} %get-tuple-element.476, f32[512,8]{0,1:T(8,128)S(1)} %get-tuple-element.477), channel_id=1, replica_groups=mesh['experts'=4,'context'=4,'dp'=2] {'experts'}, use_global_device_ids=true, to_apply=%region_22.23 | all-reduce | flops 5120 | bytes 40960 | tf_op jit(solution)/shard_map/psum | solution.py:17
  1039.7 77.2 %all-reduce.15.cloned.1.call-done = (bf16[2,512,2048]{2,1,0:T(8,128)(2,1)}, bf16[2,2048,512]{2,1,0:T(8,128)(2,1)}) async-done(((bf16[2,512,2048]{2,1,0:T(8,128)(2,1)}, bf16[2,2048,512]{2,1,0:T(8,128)(2,1)}), (bf16[2,512,2048]{2,1,0:T(8,128)(2,1)}, bf16[2,2048,512]{2,1,0:T(8,128)(2,1)})) %all-reduce.15.cloned.1.call-update) | async-done | bytes 8388624 | tf_op jit(solution)/shard_map/psum | solution.py:354
  1116.9 6.8 convert_element_type.136
  1123.7 4.6 convert_element_type.138
  1128.3 146.4 %all-reduce.13.cloned.1.call-done = (f32[512,1536]{1,0:T(8,128)}, f32[512,512]{1,0:T(8,128)}) async-done(((f32[512,1536]{1,0:T(8,128)}, f32[512,512]{1,0:T(8,128)}), (f32[512,1536]{1,0:T(8,128)}, f32[512,512]{1,0:T(8,128)})) %all-reduce.13.cloned.1.call-update) | async-done | bytes 4194320 | tf_op jit(solution)/shard_map/psum | solution.py:17
  (285 shorter events, 161.2 us)
Async XLA Ops:
  7.2 97.6 %all-gather.2.cloned.1.call-start = ((), (), s32[]{:S(2)}) async-start(), calls=%async_computation.4 | async-start | bytes 10485760 | tf_op jit(solution)/shard_map/all_gather | solution.py:180
  18.2 5.0 copy-start.60
  18.3 16.0 %copy-start.45 = (s32[32,4]{1,0:T(8,128)}, s32[32,4]{1,0:T(8,128)S(1)}, u32[]{:S(2)}) copy-start(s32[32,4]{1,0:T(8,128)S(1)} %copy.198) | copy-start | bytes 1540
  27.5 133.4 %copy-start.47 = (s32[1024]{0:T(1024)}, s32[1024]{0:T(1024)S(1)}, u32[]{:S(2)}) copy-start(s32[1024]{0:T(1024)S(1)} %fusion.96) | copy-start | bytes 12292
  34.4 82.3 %copy-start.64 = (s32[128]{0:T(128)}, s32[128]{0:T(128)S(1)}, u32[]{:S(2)}) copy-start(s32[128]{0:T(128)S(1)} %fusion.101) | copy-start | bytes 1540
  123.6 4.1 copy-start.11
  140.4 4.1 copy-start.11
  163.7 35.2 %copy-start.48 = (s32[1024]{0:T(1024)S(1)}, s32[1024]{0:T(1024)}, u32[]{:S(2)}) copy-start(s32[1024]{0:T(1024)} %copy-done.47) | copy-start | bytes 12292
  199.3 5.1 copy-start.46
  199.3 5.1 copy-start.57
  199.3 5.1 copy-start.59
  204.4 9.5 copy-start.19
  207.3 8.8 copy-start.25
  207.3 8.8 copy-start.31
  209.3 12.1 all-to-all-start
  221.4 6.5 copy-start.36
  221.4 9.6 all-to-all-start.2
  224.7 4.4 copy-start.65
  231.0 5.2 copy-start.40
  236.9 10.6 all-to-all-start.1
  247.4 9.6 all-to-all-start.3
  250.8 733.1 %all-reduce.11.cloned.1.call-start = ((), (), s32[]{:S(2)}) async-start(), calls=%async_computation.5 | async-start | bytes 8388608 | tf_op jit(solution)/shard_map/psum | solution.py:17
  270.2 3.9 copy-start.43
  270.2 3.9 copy-start.50
  270.3 3.9 copy-start.54
  274.2 4.9 copy-start.32
  289.0 4.6 copy-start.13
  289.0 4.6 copy-start.35
  299.0 7.9 copy-start.3
  299.0 7.9 copy-start.51
  308.5 8.5 copy-start.39
  317.1 9.3 copy-start.4
  341.4 6.1 copy-start.10
  350.3 8.5 copy-start.39
  358.9 9.3 copy-start.4
  383.2 6.1 copy-start.10
  401.9 497.4 %copy-start.16 = (bf16[1,1024,512]{1,2,0:T(8,128)(2,1)S(1)}, bf16[1,1024,512]{1,2,0:T(8,128)(2,1)}, u32[]{:S(2)}) copy-start(bf16[1,1024,512]{1,2,0:T(8,128)(2,1)} %copy-done.14) | copy-start | bytes 3145732
  401.9 497.4 %copy-start.56 = (f32[1024]{0:T(1024)S(1)}, f32[1024]{0:T(1024)}, u32[]{:S(2)}) copy-start(f32[1024]{0:T(1024)} %copy-done.55) | copy-start | bytes 12292
  401.9 497.4 %copy-start.62 = (f32[512]{0:T(512)S(1)}, f32[512]{0:T(512)}, u32[]{:S(2)}) copy-start(f32[512]{0:T(512)} %param.19) | copy-start | bytes 6148
  401.9 395.1 %collective-permute-start = (bf16[1024,1024]{1,0:T(8,128)(2,1)}, bf16[1024,1024]{1,0:T(8,128)(2,1)}, u32[]{:S(2)}, u32[]{:S(2)}) collective-permute-start(bf16[1024,1024]{1,0:T(8,128)(2,1)} %get-tuple-element.758), channel_id=1, source_target_pairs={{6,0},{0,2},{2,4},{4,6},{7,1},{1,3},{3,5},{5,7},{14,8},{8,10},{10,... | collective-permute-start | bytes 6291464 | tf_op jit(solution)/shard_map/while/body/eval_jaxpr/ppermute | solution.py:24
  802.0 44.1 %collective-permute-start = (bf16[1024,1024]{1,0:T(8,128)(2,1)}, bf16[1024,1024]{1,0:T(8,128)(2,1)}, u32[]{:S(2)}, u32[]{:S(2)}) collective-permute-start(bf16[1024,1024]{1,0:T(8,128)(2,1)} %get-tuple-element.758), channel_id=1, source_target_pairs={{6,0},{0,2},{2,4},{4,6},{7,1},{1,3},{3,5},{5,7},{14,8},{8,10},{10,... | collective-permute-start | bytes 6291464 | tf_op jit(solution)/shard_map/while/body/eval_jaxpr/ppermute | solution.py:24
  851.1 43.2 %collective-permute-start = (bf16[1024,1024]{1,0:T(8,128)(2,1)}, bf16[1024,1024]{1,0:T(8,128)(2,1)}, u32[]{:S(2)}, u32[]{:S(2)}) collective-permute-start(bf16[1024,1024]{1,0:T(8,128)(2,1)} %get-tuple-element.758), channel_id=1, source_target_pairs={{6,0},{0,2},{2,4},{4,6},{7,1},{1,3},{3,5},{5,7},{14,8},{8,10},{10,... | collective-permute-start | bytes 6291464 | tf_op jit(solution)/shard_map/while/body/eval_jaxpr/ppermute | solution.py:24
  904.7 5.5 copy-start.41
  904.7 212.1 %all-reduce.15.cloned.1.call-start = ((), (), s32[]{:S(2)}) async-start(), calls=%async_computation.7 | async-start | bytes 16777216 | tf_op jit(solution)/shard_map/psum | solution.py:354
  905.6 4.6 copy-start.23
  913.7 361.0 %all-reduce.13.cloned.1.call-start = ((), (), s32[]{:S(2)}) async-start(), calls=%async_computation.6 | async-start | bytes 8388608 | tf_op jit(solution)/shard_map/psum | solution.py:17
  986.2 4.0 copy-start.8
  1116.9 6.8 copy-start.26
  (36 other events, 82.5 us)
Sparse Core Ops, SparseCore 0:
  14.5 90.2 all-gather.1
  904.8 79.0 all-reduce.10
  989.2 127.5 all-reduce.14
  1119.1 155.5 all-reduce.12
